TPU v7x, 32 devices: a whole 2x2x4 slice. The times are simulated.
32 devices in a mesh: grp: 4 (over y, x), col: 8 (over z, core).
Axes of the slice: x: 2, y: 2, z: 4, core: 2. Of those that a mesh axis runs over, the one named last changes fastest.
Arguments:
- start_block: float32 [16, 8192], P(None, ('grp', 'col')), may hold values from -6 to 6
- tile_values: float32 [4, 8, 32, 256, 256], P('grp', 'col'), may hold values from 0 to 1, as said below
- tile_row: int32 [4, 8, 32], P('grp', 'col'), may hold values from 0 to 31, as said below
- tile_col: int32 [4, 8, 32], P('grp', 'col'), may hold values from 0 to 31, as said below
- tile_count: int32 [4, 8], P('grp', 'col'), may hold values from 8 to 32, as said below
Outputs:
- basis: float32 [5, 16, 8192], P(None, None, ('grp', 'col'))
- projections: float32 [4, 4, 16, 16], replicated
- factors: float32 [5, 16, 16], replicated
Inputs may be any that keep to these rules, and one draw needn't show every extreme that they name: `tile_row`: A tile of the device at grp index g lies in tile rows g * 8 * 1 to (g + 1) * 8 - 1. `tile_col`: A tile column t of the device at col index c has (t) % 8 == c. Coordinate pairs may repeat; repeated tiles add. The live tiles of a device are its first tile_count slots; some device has all 32 slots live. `tile_values`: entries are nonnegative.
All inputs are finite; a program needn't handle non-finite values.
Results may differ from a plain program's by a relative error of at most 0.0003.
Values sent between devices are 32-bit elements; how exact they have to be, the bound alone decides.
A program may use at most 64 MiB of HBM per device.

v0:
```python
import jax
import jax.numpy as jnp
from jax import lax
from jax.sharding import PartitionSpec as P

ITERS = 4


highest = lax.Precision.HIGHEST


def select_rows(selector, panel, tile_size):
    block_rows = panel.shape[0]
    shaped = panel.reshape(block_rows, -1, tile_size)
    return jnp.einsum("sr,qrt->qst", selector, shaped, precision=highest)


def spread_rows(selector, pieces):
    block_rows = pieces.shape[0]
    placed = jnp.einsum("sr,qst->qrt", selector, pieces, precision=highest)
    return placed.reshape(block_rows, -1)


def orthonormal(block_rows, gram_now):
    factor = jnp.linalg.cholesky(gram_now)
    solved = jax.scipy.linalg.solve_triangular(factor, block_rows, lower=True)
    return (solved, factor)


def body(start_block, tile_values, tile_row, tile_col, tile_count):
    grp_size = lax.axis_size("grp")
    col_size = lax.axis_size("col")
    grp_index = lax.axis_index("grp")
    tile_data = tile_values[0, 0]
    tile_size = tile_data.shape[-1]
    slot_count = tile_data.shape[0]
    shard_len = start_block.shape[1]
    row_tiles = shard_len // tile_size
    node_total = shard_len * grp_size * col_size
    live_slot = (jnp.arange(slot_count, dtype=jnp.int32) < tile_count[0, 0]).astype(jnp.float32)
    local_row = tile_row[0, 0] - grp_index * (col_size * row_tiles)
    global_col = tile_col[0, 0]
    local_col = global_col // (row_tiles * col_size) * row_tiles + global_col % row_tiles
    row_places = jnp.arange(col_size * row_tiles, dtype=jnp.int32)
    col_places = jnp.arange(grp_size * row_tiles, dtype=jnp.int32)
    row_select = (local_row[:, None] == row_places[None, :]).astype(jnp.float32) * live_slot[
        :, None
    ]
    col_select = (local_col[:, None] == col_places[None, :]).astype(jnp.float32) * live_slot[
        :, None
    ]

    def combine(part_rows, part_cols):
        mine_rows = lax.psum_scatter(part_rows, "col", scatter_dimension=1, tiled=True)
        mine_cols = lax.psum_scatter(part_cols, "grp", scatter_dimension=1, tiled=True)
        return mine_rows + mine_cols

    row_totals = jnp.sum(tile_data, axis=2)[None]
    col_totals = jnp.sum(tile_data, axis=1)[None]
    degree = combine(spread_rows(row_select, row_totals), spread_rows(col_select, col_totals))
    start_gram = (
        lax.psum(jnp.dot(start_block, start_block.T, precision=highest), ("grp", "col"))
        / node_total
    )
    first_block, factor = orthonormal(start_block, start_gram)
    block_width = start_block.shape[0]
    basis_list = [first_block]
    factor_list = [factor]
    projections = jnp.zeros((ITERS, ITERS, block_width, block_width), jnp.float32)
    for step_index in range(ITERS):
        laplace_vector = basis_list[-1]
        row_panel = lax.all_gather(laplace_vector, "col", axis=1, tiled=True)
        col_panel = lax.all_gather(laplace_vector, "grp", axis=1, tiled=True)
        at_cols = select_rows(col_select, col_panel, tile_size)
        at_rows = select_rows(row_select, row_panel, tile_size)
        into_rows = jnp.einsum("sij,qsj->qsi", tile_data, at_cols, precision=highest)
        into_cols = jnp.einsum("sij,qsi->qsj", tile_data, at_rows, precision=highest)
        product = combine(spread_rows(row_select, into_rows), spread_rows(col_select, into_cols))
        applied = degree * laplace_vector - product
        stacked = jnp.stack(basis_list)
        coeff_part = jnp.einsum("an,jbn->jab", applied, stacked, precision=highest)
        coeffs = lax.psum(coeff_part, ("grp", "col")) / node_total
        applied = applied - jnp.einsum("jab,jbn->an", coeffs, stacked, precision=highest)
        gram_now = (
            lax.psum(jnp.dot(applied, applied.T, precision=highest), ("grp", "col")) / node_total
        )
        next_block, factor = orthonormal(applied, gram_now)
        basis_list.append(next_block)
        factor_list.append(factor)
        projections = projections.at[step_index, : step_index + 1].set(coeffs)
    return (jnp.stack(basis_list), projections, jnp.stack(factor_list))


def solution(mesh):
    in_specs = (
        P(None, ("grp", "col")),
        P("grp", "col", None, None, None),
        P("grp", "col", None),
        P("grp", "col", None),
        P("grp", "col"),
    )
    out_specs = (P(None, None, ("grp", "col")), P(), P())
    return jax.shard_map(body, mesh=mesh, in_specs=in_specs, out_specs=out_specs, check_vma=False)
```

profile of v0, /device:TPU:0, one launch (start us, length us, event | category | flops | bytes accessed | tf_op | source)
XLA Modules:
  0.0 785.9 jit_solution(12459310264060773894)
XLA Ops:
  16.3 42.0 %psum.63 = f32[16,16]{0,1:T(8,128)S(1)} all-reduce(f32[16,16]{0,1:T(8,128)S(1)} %fusion.181), channel_id=1, replica_groups=mesh['grp'=4,'col'=8] {'grp','col'}, use_global_device_ids=true, to_apply=%region_0.1 | all-reduce | flops 256 | bytes 2048 | tf_op jit(solution)/shard_map/psum | solution.py:62
  62.6 14.2 %all_gather.25 = f32[16,2048]{1,0:T(8,128)S(1)} all-gather(f32[16,256]{1,0:T(8,128)S(1)} %get-tuple-element.65), channel_id=1, replica_groups=mesh['grp'=4,'col'=8] {'col'}, dimensions={1}, use_global_device_ids=true | all-gather | bytes 147456 | tf_op jit(solution)/shard_map/all_gather | solution.py:72
  95.2 9.5 %fusion.16 = f32[16,32,256]{2,0,1:T(8,128)S(1)} fusion(f32[1,1,32,256,256]{4,3,2,1,0:T(8,128)} %param.17, f32[16,32,256]{2,1,0:T(8,128)S(1)} %convolution_bitcast_fusion.7), kind=kOutput, calls=%fused_computation.16 | convolution fusion | flops 402653184 | bytes 9437184 | tf_op jit(solution)/shard_map/sij,qsj->qsi/dot_general | solution.py:76
  109.4 33.3 %reduce-scatter.15.cloned.1.call-done = f32[16,256]{1,0:T(8,128)} async-done(((f32[16,2048]{1,0:T(8,128)}), f32[16,256]{1,0:T(8,128)}) %reduce-scatter.15.cloned.1.call-update) | async-done | bytes 16400 | tf_op jit(solution)/shard_map/reduce_scatter | solution.py:54
  143.6 37.8 %psum.64 = f32[1,16,16]{1,2,0:T(8,128)S(1)} all-reduce(f32[1,16,16]{1,2,0:T(8,128)S(1)} %convolution_bitcast_fusion.15), channel_id=1, replica_groups=mesh['grp'=4,'col'=8] {'grp','col'}, use_global_device_ids=true, to_apply=%region_9.12 | all-reduce | flops 256 | bytes 2048 | tf_op jit(solution)/shard_map/psum | solution.py:82
  182.5 41.4 %psum.65 = f32[16,16]{0,1:T(8,128)S(1)} all-reduce(f32[16,16]{0,1:T(8,128)S(1)} %fusion.182), channel_id=1, replica_groups=mesh['grp'=4,'col'=8] {'grp','col'}, use_global_device_ids=true, to_apply=%region_10.13 | all-reduce | flops 256 | bytes 2048 | tf_op jit(solution)/shard_map/psum | solution.py:85
  237.2 13.9 %all_gather.27 = f32[16,2048]{1,0:T(8,128)S(1)} all-gather(f32[16,256]{1,0:T(8,128)S(1)} %get-tuple-element.67), channel_id=1, replica_groups=mesh['grp'=4,'col'=8] {'col'}, dimensions={1}, use_global_device_ids=true | all-gather | bytes 147456 | tf_op jit(solution)/shard_map/all_gather | solution.py:72
  251.8 9.5 %fusion.22 = f32[16,32,256]{2,0,1:T(8,128)S(1)} fusion(f32[1,1,32,256,256]{4,3,2,1,0:T(8,128)} %param.17, f32[16,32,256]{2,1,0:T(8,128)S(1)} %convolution_bitcast_fusion.6), kind=kOutput, calls=%fused_computation.18 | convolution fusion | flops 402653184 | bytes 9437184 | tf_op jit(solution)/shard_map/sij,qsj->qsi/dot_general | solution.py:76
  272.1 20.3 %reduce-scatter.21.cloned.1.call-done = f32[16,256]{1,0:T(8,128)} async-done(((f32[16,1024]{1,0:T(8,128)}), f32[16,256]{1,0:T(8,128)}) %reduce-scatter.21.cloned.1.call-update) | async-done | bytes 16400 | tf_op jit(solution)/shard_map/reduce_scatter | solution.py:55
  292.4 33.3 %reduce-scatter.19.cloned.1.call-done = f32[16,256]{1,0:T(8,128)} async-done(((f32[16,2048]{1,0:T(8,128)}), f32[16,256]{1,0:T(8,128)}) %reduce-scatter.19.cloned.1.call-update) | async-done | bytes 16400 | tf_op jit(solution)/shard_map/reduce_scatter | solution.py:54
  326.7 37.8 %psum.66 = f32[2,16,16]{1,2,0:T(8,128)S(1)} all-reduce(f32[2,16,16]{1,2,0:T(8,128)S(1)} %convolution_bitcast_fusion.14), channel_id=1, replica_groups=mesh['grp'=4,'col'=8] {'grp','col'}, use_global_device_ids=true, to_apply=%region_13.16 | all-reduce | flops 512 | bytes 4096 | tf_op jit(solution)/shard_map/psum | solution.py:82
  364.9 41.6 %psum.67 = f32[16,16]{0,1:T(8,128)S(1)} all-reduce(f32[16,16]{0,1:T(8,128)S(1)} %fusion.183), channel_id=1, replica_groups=mesh['grp'=4,'col'=8] {'grp','col'}, use_global_device_ids=true, to_apply=%region_14.17 | all-reduce | flops 256 | bytes 2048 | tf_op jit(solution)/shard_map/psum | solution.py:85
  419.8 13.9 %all_gather.29 = f32[16,2048]{1,0:T(8,128)S(1)} all-gather(f32[16,256]{1,0:T(8,128)S(1)} %get-tuple-element.69), channel_id=1, replica_groups=mesh['grp'=4,'col'=8] {'col'}, dimensions={1}, use_global_device_ids=true | all-gather | bytes 147456 | tf_op jit(solution)/shard_map/all_gather | solution.py:72
  434.4 9.5 %fusion.28 = f32[16,32,256]{2,0,1:T(8,128)S(1)} fusion(f32[1,1,32,256,256]{4,3,2,1,0:T(8,128)} %param.17, f32[16,32,256]{2,1,0:T(8,128)S(1)} %convolution_bitcast_fusion.5), kind=kOutput, calls=%fused_computation.20 | convolution fusion | flops 402653184 | bytes 9437184 | tf_op jit(solution)/shard_map/sij,qsj->qsi/dot_general | solution.py:76
  454.7 20.3 %reduce-scatter.25.cloned.1.call-done = f32[16,256]{1,0:T(8,128)} async-done(((f32[16,1024]{1,0:T(8,128)}), f32[16,256]{1,0:T(8,128)}) %reduce-scatter.25.cloned.1.call-update) | async-done | bytes 16400 | tf_op jit(solution)/shard_map/reduce_scatter | solution.py:55
  475.0 33.5 %reduce-scatter.23.cloned.1.call-done = f32[16,256]{1,0:T(8,128)} async-done(((f32[16,2048]{1,0:T(8,128)}), f32[16,256]{1,0:T(8,128)}) %reduce-scatter.23.cloned.1.call-update) | async-done | bytes 16400 | tf_op jit(solution)/shard_map/reduce_scatter | solution.py:54
  509.4 37.9 %psum.68 = f32[3,16,16]{1,2,0:T(8,128)S(1)} all-reduce(f32[3,16,16]{1,2,0:T(8,128)S(1)} %convolution_bitcast_fusion.9), channel_id=1, replica_groups=mesh['grp'=4,'col'=8] {'grp','col'}, use_global_device_ids=true, to_apply=%region_17.20 | all-reduce | flops 768 | bytes 6144 | tf_op jit(solution)/shard_map/psum | solution.py:82
  547.7 41.4 %psum.69 = f32[16,16]{0,1:T(8,128)S(1)} all-reduce(f32[16,16]{0,1:T(8,128)S(1)} %fusion.184), channel_id=1, replica_groups=mesh['grp'=4,'col'=8] {'grp','col'}, use_global_device_ids=true, to_apply=%region_18.21 | all-reduce | flops 256 | bytes 2048 | tf_op jit(solution)/shard_map/psum | solution.py:85
  602.5 14.2 %all_gather.31 = f32[16,2048]{1,0:T(8,128)S(1)} all-gather(f32[16,256]{1,0:T(8,128)S(1)} %get-tuple-element.71), channel_id=1, replica_groups=mesh['grp'=4,'col'=8] {'col'}, dimensions={1}, use_global_device_ids=true | all-gather | bytes 147456 | tf_op jit(solution)/shard_map/all_gather | solution.py:72
  617.3 9.5 %fusion.34 = f32[16,32,256]{2,0,1:T(8,128)S(1)} fusion(f32[1,1,32,256,256]{4,3,2,1,0:T(8,128)} %param.17, f32[16,32,256]{2,1,0:T(8,128)S(1)} %convolution_bitcast_fusion.4), kind=kOutput, calls=%fused_computation.22 | convolution fusion | flops 402653184 | bytes 9437184 | tf_op jit(solution)/shard_map/sij,qsj->qsi/dot_general | solution.py:76
  637.6 20.4 %reduce-scatter.29.cloned.1.call-done = f32[16,256]{1,0:T(8,128)} async-done(((f32[16,1024]{1,0:T(8,128)}), f32[16,256]{1,0:T(8,128)}) %reduce-scatter.29.cloned.1.call-update) | async-done | bytes 16400 | tf_op jit(solution)/shard_map/reduce_scatter | solution.py:55
  658.0 33.2 %reduce-scatter.27.cloned.1.call-done = f32[16,256]{1,0:T(8,128)} async-done(((f32[16,2048]{1,0:T(8,128)}), f32[16,256]{1,0:T(8,128)}) %reduce-scatter.27.cloned.1.call-update) | async-done | bytes 16400 | tf_op jit(solution)/shard_map/reduce_scatter | solution.py:54
  692.1 38.0 %psum.70 = f32[4,16,16]{1,2,0:T(8,128)S(1)} all-reduce(f32[4,16,16]{1,2,0:T(8,128)S(1)} %convolution_bitcast_fusion.8), channel_id=1, replica_groups=mesh['grp'=4,'col'=8] {'grp','col'}, use_global_device_ids=true, to_apply=%region_21.24 | all-reduce | flops 1024 | bytes 8192 | tf_op jit(solution)/shard_map/psum | solution.py:82
  730.5 41.3 %psum.71 = f32[16,16]{0,1:T(8,128)S(1)} all-reduce(f32[16,16]{0,1:T(8,128)S(1)} %fusion.185), channel_id=1, replica_groups=mesh['grp'=4,'col'=8] {'grp','col'}, use_global_device_ids=true, to_apply=%region_22.25 | all-reduce | flops 256 | bytes 2048 | tf_op jit(solution)/shard_map/psum | solution.py:85
  (158 shorter events, 122.3 us)
Async XLA Ops:
  7.2 9.0 %copy-start = (f32[16,256]{1,0:T(8,128)S(1)}, f32[16,256]{1,0:T(8,128)}, u32[]{:S(2)}) copy-start(f32[16,256]{1,0:T(8,128)} %param.16) | copy-start | bytes 49156
  7.2 7.3 copy-start.3
  7.2 99.8 %reduce-scatter.33.cloned.1.call-start = ((), (), s32[]{:S(2)}) async-start(), calls=%async_computation.19 | async-start | bytes 655360
  14.4 93.6 %reduce-scatter.31.cloned.1.call-start = ((), (), s32[]{:S(2)}) async-start(), calls=%async_computation.18 | async-start | bytes 1179648
  16.1 93.3 %reduce-scatter.17.cloned.1.call-start = ((), (), s32[]{:S(2)}) async-start(), calls=%async_computation.11 | async-start | bytes 81920 | tf_op jit(solution)/shard_map/reduce_scatter | solution.py:55
  85.4 57.3 %reduce-scatter.15.cloned.1.call-start = ((), (), s32[]{:S(2)}) async-start(), calls=%async_computation.10 | async-start | bytes 147456 | tf_op jit(solution)/shard_map/reduce_scatter | solution.py:54
  106.1 186.3 %reduce-scatter.21.cloned.1.call-start = ((), (), s32[]{:S(2)}) async-start(), calls=%async_computation.13 | async-start | bytes 81920 | tf_op jit(solution)/shard_map/reduce_scatter | solution.py:55
  269.9 55.8 %reduce-scatter.19.cloned.1.call-start = ((), (), s32[]{:S(2)}) async-start(), calls=%async_computation.12 | async-start | bytes 147456 | tf_op jit(solution)/shard_map/reduce_scatter | solution.py:54
  271.4 203.6 %reduce-scatter.25.cloned.1.call-start = ((), (), s32[]{:S(2)}) async-start(), calls=%async_computation.15 | async-start | bytes 81920 | tf_op jit(solution)/shard_map/reduce_scatter | solution.py:55
  452.5 56.0 %reduce-scatter.23.cloned.1.call-start = ((), (), s32[]{:S(2)}) async-start(), calls=%async_computation.14 | async-start | bytes 147456 | tf_op jit(solution)/shard_map/reduce_scatter | solution.py:54
  454.0 204.0 %reduce-scatter.29.cloned.1.call-start = ((), (), s32[]{:S(2)}) async-start(), calls=%async_computation.17 | async-start | bytes 81920 | tf_op jit(solution)/shard_map/reduce_scatter | solution.py:55
  635.5 55.7 %reduce-scatter.27.cloned.1.call-start = ((), (), s32[]{:S(2)}) async-start(), calls=%async_computation.16 | async-start | bytes 147456 | tf_op jit(solution)/shard_map/reduce_scatter | solution.py:54
  777.4 0.6 copy-start.2
  778.0 0.6 copy-start.1
Sparse Core Ops, SparseCore 0:
  14.5 27.8 reduce-scatter.32
  44.6 32.9 reduce-scatter.30
  85.6 23.7 reduce-scatter.16
  112.1 30.6 reduce-scatter.14
  270.1 22.3 reduce-scatter.20
  295.1 30.6 reduce-scatter.18
  452.7 22.3 reduce-scatter.24
  477.9 30.6 reduce-scatter.22
  635.6 22.3 reduce-scatter.28
  660.7 30.4 reduce-scatter.26
where the time goes:
time: 797 us; the launch traced here: 786 us
  blocking collectives  452 us (57%)
  waiting for transfers between devices  195 us (24%)
  matrix products  79.7 us (10%)
  other arithmetic  30.8 us (4%)
  between operations  15.8 us (2%)
  local copies, waits for them, and re-layouts  12.4 us (2%)
    psum x4, blocking collectives, body(): lax.psum(jnp.dot(applied, applied.T, precision=highest), ('grp', 'col'))  166 us
    psum x4, blocking collectives, body(): coeffs = lax.psum(coeff_part, ('grp', 'col')) / node_total  152 us
    reduce_scatter x4, waiting for transfers between devices, combine(): lax.psum_scatter(part_rows, 'col', scatter_dimension=1, tiled=True)  133 us
    reduce_scatter x4, waiting for transfers between devices, combine(): lax.psum_scatter(part_cols, 'grp', scatter_dimension=1, tiled=True)  61.4 us
    all_gather x4, blocking collectives, body(): row_panel = lax.all_gather(laplace_vector, 'col', axis=1, tiled=True)  56.3 us
    psum x1, blocking collectives, body(): lax.psum(jnp.dot(start_block, start_block.T, precision=highest), ('grp',...  42 us
    dot_general x4, matrix products, body(): jnp.einsum('sij,qsj->qsi', tile_data, at_cols, precision=highest)  37.9 us
    all_gather x4, blocking collectives, body(): col_panel = lax.all_gather(laplace_vector, 'grp', axis=1, tiled=True)  36.1 us
  transfers between devices with their start and end apart: 10, of which 8 were waited for; matrix products, arithmetic and copies ran while one was open for 4% of the time, Pallas kernels for 0%

commit v1 on v0

v1 whole, which is shorter than its diff:
```python
import functools

import jax
import jax.numpy as jnp
from jax import lax
from jax.experimental import pallas as pl
from jax.experimental.pallas import tpu as pltpu
from jax.sharding import PartitionSpec as P

ITERS = 4
HIGHEST = lax.Precision.HIGHEST
MESH = pl.DeviceIdType.MESH
F32 = jnp.float32
BF16 = jnp.bfloat16
LANES = 128


def dot_nt(left, right, precision=None):
    dims = (((1,), (1,)), ((), ()))
    return lax.dot_general(left, right, dims, precision=precision, preferred_element_type=F32)


def dot_nn(left, right, precision=None):
    dims = (((1,), (0,)), ((), ()))
    return lax.dot_general(left, right, dims, precision=precision, preferred_element_type=F32)


def split_two(value):
    high = value.astype(BF16)
    low = (value - high.astype(F32)).astype(BF16)
    return high, low


def factorize(gram):
    width = gram.shape[0]
    row = lax.broadcasted_iota(jnp.int32, gram.shape, 0)
    lane = lax.broadcasted_iota(jnp.int32, gram.shape, 1)
    unit = jnp.where(lane == row + width, 1.0, 0.0).astype(F32)
    work = jnp.where(lane < width, gram, unit)
    for j in range(width):
        column = jnp.broadcast_to(work[:, j : j + 1], work.shape)
        pivot_row = jnp.broadcast_to(work[j : j + 1, :], work.shape)
        pivot = jnp.broadcast_to(column[j : j + 1, :], work.shape)
        scale = jnp.where(row > j, column / pivot, 0.0)
        work = work - scale * pivot_row
    diagonal = jnp.sum(jnp.where(lane == row, work, 0.0), axis=1, keepdims=True)
    work = work / jnp.sqrt(diagonal)
    upper = jnp.where((lane < width) & (lane >= row), work, 0.0)
    identity = jnp.where(lane == row, 1.0, 0.0).astype(F32)
    factor = dot_nt(identity, jnp.concatenate([upper] * (LANES // width), axis=0), HIGHEST)
    return factor[:, :width], work[:, width : 2 * width]


def kernel(
    grp_size, col_size, node_total,
    start_ref, tiles_ref, row_ref, col_ref, count_ref,
    basis_ref, proj_ref, factors_ref,
    raw, high, low, q_ref, row_panel, col_panel, row_split, col_split,
    acc_row, acc_col, got_row, got_col, one_col, one_grp, two_col, two_grp,
    tile_sem, gather_row_sem, gather_col_sem, scatter_row_sem, scatter_col_sem,
    one_col_sem, one_grp_sem, two_col_sem, two_grp_sem,
):
    grp = lax.axis_index("grp")
    col = lax.axis_index("col")
    slots, tile_size = raw.shape[0], raw.shape[1]
    width = start_ref.shape[0]
    group = 4 if slots % 4 == 0 else 1

    def load_tile(s):
        return pltpu.make_async_copy(tiles_ref.at[s], raw.at[s], tile_sem.at[s])

    def start_load(s, carry):
        load_tile(s).start()
        return carry

    lax.fori_loop(0, slots, start_load, 0)

    barrier = pltpu.get_barrier_semaphore()

    def greet_col(d, carry):
        pl.semaphore_signal(
            barrier, inc=1, device_id=(grp, lax.rem(col + d, col_size)), device_id_type=MESH
        )
        return carry

    def greet_grp(d, carry):
        pl.semaphore_signal(
            barrier, inc=1, device_id=(lax.rem(grp + d, grp_size), col), device_id_type=MESH
        )
        return carry

    lax.fori_loop(1, col_size, greet_col, 0)
    lax.fori_loop(1, grp_size, greet_grp, 0)

    def exchange(axis, source, target, sems, start):
        size = col_size if axis == "col" else grp_size
        me = col if axis == "col" else grp

        def visit(d, carry):
            peer = lax.rem(me + d, size)
            copy = pltpu.make_async_remote_copy(
                src_ref=source(peer),
                dst_ref=target,
                send_sem=sems.at[0, d],
                recv_sem=sems.at[1, d],
                device_id=(grp, peer) if axis == "col" else (peer, col),
                device_id_type=MESH,
            )
            if start:
                copy.start()
            else:
                copy.wait()
            return carry

        lax.fori_loop(1, size, visit, 0, unroll=size <= 8)

    def reduce_start(part, col_buf, col_sems):
        col_buf[col] = part
        exchange("col", lambda peer: col_buf.at[col], col_buf.at[col], col_sems, True)

    def reduce_finish(col_buf, grp_buf, col_sems, grp_sems):
        exchange("col", lambda peer: col_buf.at[col], col_buf.at[col], col_sems, False)
        grp_buf[grp] = jnp.sum(col_buf[...], axis=0)
        exchange("grp", lambda peer: grp_buf.at[grp], grp_buf.at[grp], grp_sems, True)
        exchange("grp", lambda peer: grp_buf.at[grp], grp_buf.at[grp], grp_sems, False)
        return jnp.sum(grp_buf[...], axis=0) / node_total

    def gram_part(block):
        return dot_nt(block, jnp.concatenate([block] * (LANES // width), axis=0), HIGHEST)

    def scatter(start):
        exchange("col", lambda peer: acc_row.at[peer], got_row.at[col], scatter_row_sem, start)
        exchange("grp", lambda peer: acc_col.at[peer], got_col.at[grp], scatter_col_sem, start)

    def scatter_total():
        got_row[col] = acc_row[col]
        got_col[grp] = acc_col[grp]
        return jnp.sum(got_row[...], axis=0) + jnp.sum(got_col[...], axis=0)

    def add_tiles(pieces_of):
        acc_row[...] = jnp.zeros_like(acc_row)
        acc_col[...] = jnp.zeros_like(acc_col)

        def visit(n, carry):
            rows, cols, into_rows, into_cols, lives = [], [], [], [], []
            for u in range(group):
                s = n * group + u
                r = jnp.clip(row_ref[s] - grp * col_size, 0, col_size - 1)
                c = jnp.clip(lax.div(col_ref[s], col_size), 0, grp_size - 1)
                into_row, into_col = pieces_of(s, r, c)
                rows.append(r)
                cols.append(c)
                lives.append(jnp.where(s < count_ref[0], 1.0, 0.0).astype(F32))
                into_rows.append(into_row)
                into_cols.append(into_col)
            for size, acc, places, pieces in (
                (col_size, acc_row, rows, into_rows),
                (grp_size, acc_col, cols, into_cols),
            ):
                for place in range(size):
                    total = acc[place]
                    for u in range(group):
                        total = total + jnp.where(places[u] == place, lives[u], 0.0) * pieces[u]
                    acc[place] = total
            return carry

        lax.fori_loop(0, slots // group, visit, 0)

    ones = jnp.ones((width, tile_size), BF16)

    def degree_pieces(s, r, c):
        load_tile(s).wait()
        first, second = split_two(raw[s])
        high[s] = first
        low[s] = second
        into_row = dot_nt(ones, first) + dot_nt(ones, second)
        into_col = dot_nn(ones, first) + dot_nn(ones, second)
        return into_row, into_col

    def product_pieces(s, r, c):
        first, second = high[s], low[s]
        at_col, at_row = col_split[c], row_split[r]
        into_row = dot_nt(at_col, first)
        into_row = into_row[:width] + into_row[width:] + dot_nt(at_col[:width], second)
        into_col = dot_nn(at_row, first)
        into_col = into_col[:width] + into_col[width:] + dot_nn(at_row[:width], second)
        return into_row, into_col

    q_ref[...] = jnp.zeros_like(q_ref)
    proj_ref[...] = jnp.zeros_like(proj_ref)
    start_part = gram_part(start_ref[...])
    pl.semaphore_wait(barrier, col_size + grp_size - 2)
    reduce_start(start_part, two_col, two_col_sem)
    add_tiles(degree_pieces)
    scatter(True)
    gram = reduce_finish(two_col, two_grp, two_col_sem, two_grp_sem)
    factor, inverse = factorize(gram)
    factors_ref[0] = factor
    q_ref[0] = dot_nn(inverse, start_ref[...], HIGHEST)
    scatter(False)
    degree = scatter_total()

    def step(k, carry):
        exchange("col", lambda peer: q_ref.at[k], row_panel.at[col], gather_row_sem, True)
        exchange("grp", lambda peer: q_ref.at[k], col_panel.at[grp], gather_col_sem, True)
        newest = q_ref[k]
        row_panel[col] = newest
        col_panel[grp] = newest
        exchange("grp", lambda peer: q_ref.at[k], col_panel.at[grp], gather_col_sem, False)
        exchange("col", lambda peer: q_ref.at[k], row_panel.at[col], gather_row_sem, False)
        for size, panel, halves in (
            (grp_size, col_panel, col_split),
            (col_size, row_panel, row_split),
        ):
            for place in range(size):
                first, second = split_two(panel[place])
                halves[place, :width] = first
                halves[place, width:] = second
        add_tiles(product_pieces)
        scatter(True)
        scatter(False)
        applied = degree * newest - scatter_total()
        stacked = q_ref[...].reshape(-1, tile_size)
        reduce_start(dot_nt(applied, stacked, HIGHEST), one_col, one_col_sem)
        coeffs = reduce_finish(one_col, one_grp, one_col_sem, one_grp_sem)
        for j in range(ITERS):
            proj_ref[k, j] = coeffs[:, j * width : (j + 1) * width]
        residual = applied - dot_nn(coeffs, stacked, HIGHEST)
        reduce_start(gram_part(residual), two_col, two_col_sem)
        gram_now = reduce_finish(two_col, two_grp, two_col_sem, two_grp_sem)
        factor_now, inverse_now = factorize(gram_now)
        factors_ref[k + 1] = factor_now
        q_ref[k + 1] = dot_nn(inverse_now, residual, HIGHEST)
        return carry

    lax.fori_loop(0, ITERS, step, 0)
    basis_ref[...] = q_ref[: ITERS + 1]


def solution(mesh):
    grp_size, col_size = mesh.shape["grp"], mesh.shape["col"]

    def body(start_block, tile_values, tile_row, tile_col, tile_count):
        width, shard_len = start_block.shape
        slots, tile_size = tile_values.shape[2], tile_values.shape[3]
        assert shard_len == tile_size and LANES % width == 0
        places = LANES // width
        node_total = shard_len * grp_size * col_size
        vmem = pl.BlockSpec(memory_space=pltpu.VMEM)
        smem = pl.BlockSpec(memory_space=pltpu.SMEM)
        block = (width, tile_size)
        small = (width, LANES)

        def sems(size):
            return pltpu.SemaphoreType.DMA((2, size))

        return pl.pallas_call(
            functools.partial(kernel, grp_size, col_size, node_total),
            out_shape=(
                jax.ShapeDtypeStruct((ITERS + 1,) + block, F32),
                jax.ShapeDtypeStruct((ITERS, ITERS, width, width), F32),
                jax.ShapeDtypeStruct((ITERS + 1, width, width), F32),
            ),
            in_specs=[vmem, pl.BlockSpec(memory_space=pl.ANY), smem, smem, smem],
            out_specs=(vmem, vmem, vmem),
            scratch_shapes=[
                pltpu.VMEM((slots, tile_size, tile_size), F32),
                pltpu.VMEM((slots, tile_size, tile_size), BF16),
                pltpu.VMEM((slots, tile_size, tile_size), BF16),
                pltpu.VMEM((places,) + block, F32),
                pltpu.VMEM((col_size,) + block, F32),
                pltpu.VMEM((grp_size,) + block, F32),
                pltpu.VMEM((col_size, 2 * width, tile_size), BF16),
                pltpu.VMEM((grp_size, 2 * width, tile_size), BF16),
                pltpu.VMEM((col_size,) + block, F32),
                pltpu.VMEM((grp_size,) + block, F32),
                pltpu.VMEM((col_size,) + block, F32),
                pltpu.VMEM((grp_size,) + block, F32),
                pltpu.VMEM((col_size,) + small, F32),
                pltpu.VMEM((grp_size,) + small, F32),
                pltpu.VMEM((col_size,) + small, F32),
                pltpu.VMEM((grp_size,) + small, F32),
                pltpu.SemaphoreType.DMA((slots,)),
                sems(col_size), sems(grp_size), sems(col_size), sems(grp_size),
                sems(col_size), sems(grp_size), sems(col_size), sems(grp_size),
            ],
            compiler_params=pltpu.CompilerParams(
                collective_id=0, has_side_effects=True, vmem_limit_bytes=40 * 1024 * 1024
            ),
        )(
            start_block,
            tile_values.reshape(slots, tile_size, tile_size),
            tile_row.reshape(slots),
            tile_col.reshape(slots),
            tile_count.reshape(1),
        )

    in_specs = (
        P(None, ("grp", "col")),
        P("grp", "col", None, None, None),
        P("grp", "col", None),
        P("grp", "col", None),
        P("grp", "col"),
    )
    out_specs = (P(None, None, ("grp", "col")), P(), P())
    return jax.shard_map(body, mesh=mesh, in_specs=in_specs, out_specs=out_specs, check_vma=False)
```

time: 797 us -> 149 us (0.19); the launches traced: 786 us -> 149 us
  blocking collectives: 452 us -> 0 us
  waiting for transfers between devices: 195 us -> 0 us
  Pallas kernels: 0 us -> 140 us
  matrix products: 79.7 us -> 0 us
  other arithmetic: 30.8 us -> 0 us
  between operations: 15.8 us -> 1.3 us
    psum x9 -> x0, blocking collectives: 359 us -> none  [the longest x4 166 us: body(): lax.psum(jnp.dot(applied, applied.T, precision=highest), ('grp', 'col'))]
    reduce_scatter x8 -> x0, waiting for transfers between devices: 195 us -> none  [the longest x4 133 us: combine(): lax.psum_scatter(part_rows, 'col', scatter_dimension=1, tiled=True)]
    pallas_call x0 -> x1, Pallas kernels: none -> 140 us  [body(): pl.pallas_call(functools.partial(kernel, grp_size, col_size, node_total),...]
    all_gather x8 -> x0, blocking collectives: 92.4 us -> none  [the longest x4 56.3 us: body(): row_panel = lax.all_gather(laplace_vector, 'col', axis=1, tiled=True)]
    dot_general x39 -> x0, matrix products: 78.7 us -> none  [the longest x4 37.9 us: body(): jnp.einsum('sij,qsj->qsi', tile_data, at_cols, precision=highest)]
    another operation x27 -> x0, other arithmetic: 20.7 us -> none  [the longest x15 10.6 us: orthonormal(): factor = jnp.linalg.cholesky(gram_now)]
  transfers between devices with their start and end apart: 10 -> 0, of which waited for: 8 -> 0; matrix products, arithmetic and copies ran while one was open for 4% -> 0% of each run, Pallas kernels for 0% -> 0%
where the time goes in v1:
time: 149 us
  Pallas kernels  140 us (94%)
  local copies, waits for them, and re-layouts  7.31 us (5%)
    pallas_call x1, Pallas kernels, body(): pl.pallas_call(functools.partial(kernel, grp_size, col_size, node_total),...  140 us
    unnamed x11, local copies, waits for them, and re-layouts  7.31 us

profile of v1, /device:TPU:0, one launch (start us, length us, event | category | flops | bytes accessed | tf_op | source)
XLA Modules:
  0.0 148.9 jit_solution(5936797565616191632)
XLA Ops:
  1.3 0.0 copy-start
  1.3 3.4 %copy-done = f32[1,1,32,256,256]{4,3,2,1,0:T(8,128)S(1)} copy-done((f32[1,1,32,256,256]{4,3,2,1,0:T(8,128)S(1)}, f32[1,1,32,256,256]{4,3,2,1,0:T(8,128)}, u32[]{:S(2)}) %copy-start) | copy-done | bytes 8388632
  4.7 0.0 copy-start.1
  4.7 0.7 copy-done.1
  5.4 0.0 copy-start.2
  5.4 0.7 copy-done.2
  6.0 0.0 copy-start.3
  6.0 0.7 copy-done.3
  6.7 140.3 %shard_map.76 = (f32[5,16,256]{2,1,0:T(8,128)S(1)}, f32[4,4,16,16]{3,2,1,0:T(8,128)S(1)}, f32[5,16,16]{2,1,0:T(8,128)S(1)}) custom-call(f32[16,256]{1,0:T(8,128)S(1)} %copy-done.1, f32[32,256,256]{2,1,0:T(8,128)S(1)} %bitcast.5, s32[32]{0:T(128)S(1)} %bitcast.6, s32[32]{0:T(128)S(1)} %bitcast.7, s32[1]{0:T(128)} %bitcast.4.count_ref), custom_call_target="tpu_custom_call" | custom-call | tf_op jit(solution)/shard_map/pallas_call | solution.py:257
  147.0 0.6 copy.12
  147.7 0.7 copy.13
  148.3 0.6 copy.14
Async XLA Ops:
  1.3 3.4 %copy-start = (f32[1,1,32,256,256]{4,3,2,1,0:T(8,128)S(1)}, f32[1,1,32,256,256]{4,3,2,1,0:T(8,128)}, u32[]{:S(2)}) copy-start(f32[1,1,32,256,256]{4,3,2,1,0:T(8,128)} %param.6) | copy-start | bytes 25165828
  4.7 0.7 copy-start.1
  5.4 0.7 copy-start.2
  6.0 0.7 copy-start.3

commit v2 on v1

--- a/solution.py
+++ b/solution.py
@@ -56,8 +56,10 @@
     start_ref, tiles_ref, row_ref, col_ref, count_ref,
     basis_ref, proj_ref, factors_ref,
     raw, high, low, q_ref, row_panel, col_panel, row_split, col_split,
-    acc_row, acc_col, got_row, got_col, one_col, one_grp, two_col, two_grp,
+    acc_row, acc_col, got_row, got_col, deg_row, deg_col, deg_got_row, deg_got_col,
+    degree_ref, r_ref, one_col, one_grp, two_col, two_grp,
     tile_sem, gather_row_sem, gather_col_sem, scatter_row_sem, scatter_col_sem,
+    deg_row_sem, deg_col_sem,
     one_col_sem, one_grp_sem, two_col_sem, two_grp_sem,
 ):
     grp = lax.axis_index("grp")
@@ -118,28 +120,34 @@
         col_buf[col] = part
         exchange("col", lambda peer: col_buf.at[col], col_buf.at[col], col_sems, True)
 
-    def reduce_finish(col_buf, grp_buf, col_sems, grp_sems):
+    def reduce_turn(col_buf, grp_buf, col_sems, grp_sems):
         exchange("col", lambda peer: col_buf.at[col], col_buf.at[col], col_sems, False)
         grp_buf[grp] = jnp.sum(col_buf[...], axis=0)
         exchange("grp", lambda peer: grp_buf.at[grp], grp_buf.at[grp], grp_sems, True)
+
+    def reduce_end(grp_buf, grp_sems):
         exchange("grp", lambda peer: grp_buf.at[grp], grp_buf.at[grp], grp_sems, False)
         return jnp.sum(grp_buf[...], axis=0) / node_total
 
     def gram_part(block):
         return dot_nt(block, jnp.concatenate([block] * (LANES // width), axis=0), HIGHEST)
 
-    def scatter(start):
-        exchange("col", lambda peer: acc_row.at[peer], got_row.at[col], scatter_row_sem, start)
-        exchange("grp", lambda peer: acc_col.at[peer], got_col.at[grp], scatter_col_sem, start)
-
-    def scatter_total():
-        got_row[col] = acc_row[col]
-        got_col[grp] = acc_col[grp]
-        return jnp.sum(got_row[...], axis=0) + jnp.sum(got_col[...], axis=0)
-
-    def add_tiles(pieces_of):
-        acc_row[...] = jnp.zeros_like(acc_row)
-        acc_col[...] = jnp.zeros_like(acc_col)
+    def scatter(rows, cols, row_in, col_in, row_sems, col_sems, start):
+        exchange("col", lambda peer: rows.at[peer], row_in.at[col], row_sems, start)
+        exchange("grp", lambda peer: cols.at[peer], col_in.at[grp], col_sems, start)
+
+    def total_of(rows, cols, row_in, col_in):
+        row_in[col] = rows[col]
+        col_in[grp] = cols[grp]
+        return jnp.sum(row_in[...], axis=0) + jnp.sum(col_in[...], axis=0)
+
+    def gather(start):
+        exchange("col", lambda peer: r_ref, row_panel.at[col], gather_row_sem, start)
+        exchange("grp", lambda peer: r_ref, col_panel.at[grp], gather_col_sem, start)
+
+    def add_tiles(pieces_of, sum_rows, sum_cols):
+        sum_rows[...] = jnp.zeros_like(sum_rows)
+        sum_cols[...] = jnp.zeros_like(sum_cols)
 
         def visit(n, carry):
             rows, cols, into_rows, into_cols, lives = [], [], [], [], []
@@ -154,8 +162,8 @@
                 into_rows.append(into_row)
                 into_cols.append(into_col)
             for size, acc, places, pieces in (
-                (col_size, acc_row, rows, into_rows),
-                (grp_size, acc_col, cols, into_cols),
+                (col_size, sum_rows, rows, into_rows),
+                (grp_size, sum_cols, cols, into_cols),
             ):
                 for place in range(size):
                     total = acc[place]
@@ -186,28 +194,32 @@
         into_col = into_col[:width] + into_col[width:] + dot_nn(at_row[:width], second)
         return into_row, into_col
 
+    degree_refs = (deg_row, deg_col, deg_got_row, deg_got_col)
+    product_refs = (acc_row, acc_col, got_row, got_col)
+    degree_sems = (deg_row_sem, deg_col_sem)
+    product_sems = (scatter_row_sem, scatter_col_sem)
+
+    def next_block(k, gram):
+        factor, inverse = factorize(gram)
+        factors_ref[k] = factor
+        q_ref[k] = dot_nn(inverse, r_ref[...], HIGHEST)
+        return inverse
+
     q_ref[...] = jnp.zeros_like(q_ref)
     proj_ref[...] = jnp.zeros_like(proj_ref)
+    r_ref[...] = start_ref[...]
     start_part = gram_part(start_ref[...])
     pl.semaphore_wait(barrier, col_size + grp_size - 2)
     reduce_start(start_part, two_col, two_col_sem)
-    add_tiles(degree_pieces)
-    scatter(True)
-    gram = reduce_finish(two_col, two_grp, two_col_sem, two_grp_sem)
-    factor, inverse = factorize(gram)
-    factors_ref[0] = factor
-    q_ref[0] = dot_nn(inverse, start_ref[...], HIGHEST)
-    scatter(False)
-    degree = scatter_total()
+    gather(True)
+    add_tiles(degree_pieces, deg_row, deg_col)
+    scatter(*degree_refs, *degree_sems, True)
 
     def step(k, carry):
-        exchange("col", lambda peer: q_ref.at[k], row_panel.at[col], gather_row_sem, True)
-        exchange("grp", lambda peer: q_ref.at[k], col_panel.at[grp], gather_col_sem, True)
-        newest = q_ref[k]
+        newest = r_ref[...]
         row_panel[col] = newest
         col_panel[grp] = newest
-        exchange("grp", lambda peer: q_ref.at[k], col_panel.at[grp], gather_col_sem, False)
-        exchange("col", lambda peer: q_ref.at[k], row_panel.at[col], gather_row_sem, False)
+        gather(False)
         for size, panel, halves in (
             (grp_size, col_panel, col_split),
             (col_size, row_panel, row_split),
@@ -216,24 +228,38 @@
                 first, second = split_two(panel[place])
                 halves[place, :width] = first
                 halves[place, width:] = second
-        add_tiles(product_pieces)
-        scatter(True)
-        scatter(False)
-        applied = degree * newest - scatter_total()
+        add_tiles(product_pieces, acc_row, acc_col)
+        scatter(*product_refs, *product_sems, True)
+        reduce_turn(two_col, two_grp, two_col_sem, two_grp_sem)
+
+        @pl.when(k == 0)
+        def _():
+            scatter(*degree_refs, *degree_sems, False)
+            degree_ref[...] = total_of(*degree_refs)
+
+        inverse = next_block(k, reduce_end(two_grp, two_grp_sem))
+        scatter(*product_refs, *product_sems, False)
+        laplace = degree_ref[...] * newest - total_of(*product_refs)
+        applied = dot_nn(inverse, laplace, HIGHEST)
         stacked = q_ref[...].reshape(-1, tile_size)
         reduce_start(dot_nt(applied, stacked, HIGHEST), one_col, one_col_sem)
-        coeffs = reduce_finish(one_col, one_grp, one_col_sem, one_grp_sem)
+        reduce_turn(one_col, one_grp, one_col_sem, one_grp_sem)
+        coeffs = reduce_end(one_grp, one_grp_sem)
         for j in range(ITERS):
             proj_ref[k, j] = coeffs[:, j * width : (j + 1) * width]
         residual = applied - dot_nn(coeffs, stacked, HIGHEST)
+        r_ref[...] = residual
+
+        @pl.when(k < ITERS - 1)
+        def _():
+            gather(True)
+
         reduce_start(gram_part(residual), two_col, two_col_sem)
-        gram_now = reduce_finish(two_col, two_grp, two_col_sem, two_grp_sem)
-        factor_now, inverse_now = factorize(gram_now)
-        factors_ref[k + 1] = factor_now
-        q_ref[k + 1] = dot_nn(inverse_now, residual, HIGHEST)
         return carry
 
     lax.fori_loop(0, ITERS, step, 0)
+    reduce_turn(two_col, two_grp, two_col_sem, two_grp_sem)
+    next_block(ITERS, reduce_end(two_grp, two_grp_sem))
     basis_ref[...] = q_ref[: ITERS + 1]
 
 
@@ -276,12 +302,19 @@
                 pltpu.VMEM((grp_size,) + block, F32),
                 pltpu.VMEM((col_size,) + block, F32),
                 pltpu.VMEM((grp_size,) + block, F32),
+                pltpu.VMEM((col_size,) + block, F32),
+                pltpu.VMEM((grp_size,) + block, F32),
+                pltpu.VMEM((col_size,) + block, F32),
+                pltpu.VMEM((grp_size,) + block, F32),
+                pltpu.VMEM(block, F32),
+                pltpu.VMEM(block, F32),
                 pltpu.VMEM((col_size,) + small, F32),
                 pltpu.VMEM((grp_size,) + small, F32),
                 pltpu.VMEM((col_size,) + small, F32),
                 pltpu.VMEM((grp_size,) + small, F32),
                 pltpu.SemaphoreType.DMA((slots,)),
                 sems(col_size), sems(grp_size), sems(col_size), sems(grp_size),
+                sems(col_size), sems(grp_size),
                 sems(col_size), sems(grp_size), sems(col_size), sems(grp_size),
             ],
             compiler_params=pltpu.CompilerParams(

time: 149 us -> 118 us (0.79)
  Pallas kernels: 140 us -> 109 us
    pallas_call x1, Pallas kernels: 140 us -> 109 us  [body(): pl.pallas_call(functools.partial(kernel, grp_size, col_size, node_total),...]
where the time goes in v2:
time: 118 us
  Pallas kernels  109 us (92%)
  local copies, waits for them, and re-layouts  7.31 us (6%)
  between operations  1.3 us (1%)
    pallas_call x1, Pallas kernels, body(): pl.pallas_call(functools.partial(kernel, grp_size, col_size, node_total),...  109 us
    unnamed x11, local copies, waits for them, and re-layouts  7.31 us

profile of v2, /device:TPU:0, one launch (start us, length us, event | category | flops | bytes accessed | tf_op | source)
XLA Modules:
  0.0 118.1 jit_solution(4382237571502338892)
XLA Ops:
  1.3 0.0 copy-start
  1.3 3.4 %copy-done = f32[1,1,32,256,256]{4,3,2,1,0:T(8,128)S(1)} copy-done((f32[1,1,32,256,256]{4,3,2,1,0:T(8,128)S(1)}, f32[1,1,32,256,256]{4,3,2,1,0:T(8,128)}, u32[]{:S(2)}) %copy-start) | copy-done | bytes 8388632
  4.7 0.0 copy-start.1
  4.7 0.7 copy-done.1
  5.4 0.0 copy-start.2
  5.4 0.7 copy-done.2
  6.0 0.0 copy-start.3
  6.0 0.7 copy-done.3
  6.7 109.5 %shard_map.76 = (f32[5,16,256]{2,1,0:T(8,128)S(1)}, f32[4,4,16,16]{3,2,1,0:T(8,128)S(1)}, f32[5,16,16]{2,1,0:T(8,128)S(1)}) custom-call(f32[16,256]{1,0:T(8,128)S(1)} %copy-done.1, f32[32,256,256]{2,1,0:T(8,128)S(1)} %bitcast.5, s32[32]{0:T(128)S(1)} %bitcast.6, s32[32]{0:T(128)S(1)} %bitcast.7, s32[1]{0:T(128)} %bitcast.4.count_ref), custom_call_target="tpu_custom_call" | custom-call | tf_op jit(solution)/shard_map/pallas_call | solution.py:283
  116.2 0.6 copy.12
  116.8 0.7 copy.13
  117.5 0.6 copy.14
Async XLA Ops:
  1.3 3.4 %copy-start = (f32[1,1,32,256,256]{4,3,2,1,0:T(8,128)S(1)}, f32[1,1,32,256,256]{4,3,2,1,0:T(8,128)}, u32[]{:S(2)}) copy-start(f32[1,1,32,256,256]{4,3,2,1,0:T(8,128)} %param.6) | copy-start | bytes 25165828
  4.7 0.7 copy-start.1
  5.4 0.7 copy-start.2
  6.0 0.7 copy-start.3

commit v3 on v2

--- a/solution.py
+++ b/solution.py
@@ -228,9 +228,9 @@
                 first, second = split_two(panel[place])
                 halves[place, :width] = first
                 halves[place, width:] = second
+        reduce_turn(two_col, two_grp, two_col_sem, two_grp_sem)
         add_tiles(product_pieces, acc_row, acc_col)
         scatter(*product_refs, *product_sems, True)
-        reduce_turn(two_col, two_grp, two_col_sem, two_grp_sem)
 
         @pl.when(k == 0)
         def _():
@@ -245,8 +245,6 @@
         reduce_start(dot_nt(applied, stacked, HIGHEST), one_col, one_col_sem)
         reduce_turn(one_col, one_grp, one_col_sem, one_grp_sem)
         coeffs = reduce_end(one_grp, one_grp_sem)
-        for j in range(ITERS):
-            proj_ref[k, j] = coeffs[:, j * width : (j + 1) * width]
         residual = applied - dot_nn(coeffs, stacked, HIGHEST)
         r_ref[...] = residual
 
@@ -255,6 +253,8 @@
             gather(True)
 
         reduce_start(gram_part(residual), two_col, two_col_sem)
+        for j in range(ITERS):
+            proj_ref[k, j] = coeffs[:, j * width : (j + 1) * width]
         return carry
 
     lax.fori_loop(0, ITERS, step, 0)

time: 118 us -> 116 us (0.983)
  Pallas kernels: 109 us -> 107 us
    pallas_call x1, Pallas kernels: 109 us -> 107 us  [body(): pl.pallas_call(functools.partial(kernel, grp_size, col_size, node_total),...]
where the time goes in v3:
time: 116 us
  Pallas kernels  107 us (92%)
  local copies, waits for them, and re-layouts  7.31 us (6%)
  between operations  1.3 us (1%)
    pallas_call x1, Pallas kernels, body(): pl.pallas_call(functools.partial(kernel, grp_size, col_size, node_total),...  107 us
    unnamed x11, local copies, waits for them, and re-layouts  7.31 us

profile of v3, /device:TPU:0, one launch (start us, length us, event | category | flops | bytes accessed | tf_op | source)
XLA Modules:
  0.0 115.6 jit_solution(3807898196832445446)
XLA Ops:
  1.3 0.0 copy-start
  1.3 3.4 %copy-done = f32[1,1,32,256,256]{4,3,2,1,0:T(8,128)S(1)} copy-done((f32[1,1,32,256,256]{4,3,2,1,0:T(8,128)S(1)}, f32[1,1,32,256,256]{4,3,2,1,0:T(8,128)}, u32[]{:S(2)}) %copy-start) | copy-done | bytes 8388632
  4.7 0.0 copy-start.1
  4.7 0.7 copy-done.1
  5.4 0.0 copy-start.2
  5.4 0.7 copy-done.2
  6.0 0.0 copy-start.3
  6.0 0.7 copy-done.3
  6.7 107.0 %shard_map.76 = (f32[5,16,256]{2,1,0:T(8,128)S(1)}, f32[4,4,16,16]{3,2,1,0:T(8,128)S(1)}, f32[5,16,16]{2,1,0:T(8,128)S(1)}) custom-call(f32[16,256]{1,0:T(8,128)S(1)} %copy-done.1, f32[32,256,256]{2,1,0:T(8,128)S(1)} %bitcast.5, s32[32]{0:T(128)S(1)} %bitcast.6, s32[32]{0:T(128)S(1)} %bitcast.7, s32[1]{0:T(128)} %bitcast.4.count_ref), custom_call_target="tpu_custom_call" | custom-call | tf_op jit(solution)/shard_map/pallas_call | solution.py:283
  113.7 0.6 copy.12
  114.3 0.7 copy.13
  115.0 0.6 copy.14
Async XLA Ops:
  1.3 3.4 %copy-start = (f32[1,1,32,256,256]{4,3,2,1,0:T(8,128)S(1)}, f32[1,1,32,256,256]{4,3,2,1,0:T(8,128)}, u32[]{:S(2)}) copy-start(f32[1,1,32,256,256]{4,3,2,1,0:T(8,128)} %param.6) | copy-start | bytes 25165828
  4.7 0.7 copy-start.1
  5.4 0.7 copy-start.2
  6.0 0.7 copy-start.3
